TPU v7x, 32 devices: a whole 2x2x4 slice. The times are simulated.
32 devices in a mesh: group: 2 (over y), exp: 4 (over z), tok: 4 (over x, core).
Axes of the slice: x: 2, y: 2, z: 4, core: 2. Of those that a mesh axis runs over, the one named last changes fastest.
Arguments:
- activations: bfloat16 [1024, 2048], P(('group', 'exp'), 'tok'), parts along dimension 0, may hold values from -6 to 6
- expert_ids: int32 [1024, 4], P(('group', 'exp')), parts along dimension 0, may hold values from 0 to 7, all different within a row; in each aligned block of 128 rows (0 to 127, 128 to 255, ...) at most 128 rows name the same one
- gate_values: float32 [1024, 4], P(('group', 'exp')), parts along dimension 0, may hold values from 0.2 to 1
- expert_gate: bfloat16 [8, 2048, 512], P('exp', 'tok'), may hold values from -0.125 to 0.125
- expert_up: bfloat16 [8, 2048, 512], P('exp', 'tok'), may hold values from -0.125 to 0.125
- expert_down: bfloat16 [8, 512, 2048], P('exp', None, 'tok'), may hold values from -0.25 to 0.25
Outputs:
- layer_out: bfloat16 [1024, 2048], P(('group', 'exp'), 'tok'), parts along dimension 0
There are 2 independent parts, one for each index of `group`. A program takes and returns all parts, laid end to end along the dimension named above; an argument that names none is the same for every part. Nothing has to cross between parts.
Inputs may be any that keep to these rules, and one draw needn't show every extreme that they name: `expert_ids`: each row names 4 different experts. Within each aligned block of 128 rows (the tokens of one index of exp) no expert is named by more than 128 rows, and in every draw some expert is named by exactly 128 rows of some block.
All inputs are finite; a program needn't handle non-finite values.
Results may differ from a plain program's by a relative error of at most 0.023.
Values may be sent and summed in bfloat16 or wider, within the bound.
A program may use at most 64 MiB of HBM per device.

v0:
```python
import jax
import jax.numpy as jnp
from jax import lax
from jax.sharding import PartitionSpec as P


def slot_positions(expert_ids, experts_all, capacity):
    flat_ids = expert_ids.reshape(-1)
    one_hot = (flat_ids[:, None] == jnp.arange(experts_all, dtype=jnp.int32)[None, :]).astype(
        jnp.int32
    )
    earlier = jnp.cumsum(one_hot, axis=0) - one_hot
    rank_within = jnp.sum(earlier * one_hot, axis=1)
    return flat_ids * capacity + rank_within


def move_rows(buffer):
    return lax.all_to_all(buffer, "exp", split_axis=0, concat_axis=0, tiled=True)


def shards(activations, expert_ids, gate_values, expert_gate, expert_up, expert_down):
    row_count, feature_cols = activations.shape
    top_count = expert_ids.shape[1]
    local_experts = expert_gate.shape[0]
    groups = lax.axis_size("exp")
    experts_all = local_experts * groups
    capacity = 2 * row_count * top_count // experts_all
    slot_index = slot_positions(expert_ids, experts_all, capacity)
    picked = jnp.repeat(activations, top_count, axis=0)
    outgoing = (
        jnp.zeros((experts_all * capacity, feature_cols), jnp.bfloat16).at[slot_index].set(picked)
    )
    arrived = move_rows(outgoing.reshape(groups, local_experts, capacity, feature_cols))
    gate_part = jnp.einsum(
        "sxcf,xfh->sxch", arrived, expert_gate, preferred_element_type=jnp.float32
    )
    up_part = jnp.einsum("sxcf,xfh->sxch", arrived, expert_up, preferred_element_type=jnp.float32)
    gate_pre, up_pre = (
        lax.psum(gate_part.astype(jnp.bfloat16), "tok").astype(jnp.float32),
        lax.psum(up_part.astype(jnp.bfloat16), "tok").astype(jnp.float32),
    )
    hidden = (jax.nn.silu(gate_pre) * up_pre).astype(jnp.bfloat16)
    results = jnp.einsum(
        "sxch,xhf->sxcf", hidden, expert_down, preferred_element_type=jnp.float32
    ).astype(jnp.bfloat16)
    returned = move_rows(results).reshape(experts_all * capacity, feature_cols)
    fetched = returned[slot_index].astype(jnp.float32).reshape(row_count, top_count, feature_cols)
    combined = jnp.sum(fetched * gate_values[:, :, None], axis=1)
    return combined.astype(jnp.bfloat16)


def solution(mesh):
    placed = (
        P(("group", "exp"), "tok"),
        P(("group", "exp"), None),
        P(("group", "exp"), None),
        P("exp", "tok", None),
        P("exp", "tok", None),
        P("exp", None, "tok"),
    )
    return jax.shard_map(
        shards, mesh=mesh, in_specs=placed, out_specs=P(("group", "exp"), "tok"), check_vma=False
    )
```

profile of v0, /device:TPU:0, one launch (start us, length us, event | category | flops | bytes accessed | tf_op | source)
XLA Modules:
  0.0 144.1 jit_solution(17230130679026216013)
XLA Ops:
  6.5 0.0 copy-start
  6.5 0.0 all-reduce.3.cloned.1.call-start
  6.5 0.9 copy.15
  7.4 0.1 eq.29
  7.5 0.1 eq.25
  7.6 0.7 broadcast_multiply_fusion
  8.3 1.1 reduce-window.6
  9.5 0.2 slice_reduce_fusion
  9.7 0.1 copy.14
  9.8 0.1 mul.36
  9.9 1.0 broadcast_in_dim.5
  11.0 0.1 reshape.77
  11.1 0.1 fusion.17
  11.2 2.7 %scatter_custom_fusion = bf16[1024,512]{1,0:T(8,128)(2,1)S(1)} fusion(s32[512]{0:T(512)S(1)} %bitcast.35, bf16[512,512]{1,0:T(8,128)(2,1)S(1)} %reshape.77, bf16[]{:T(256)} %constant.6.clone.1), kind=kCustom, calls=%fused_computation.21 | custom fusion | bytes 1048578 | tf_op jit(solution)/shard_map/scatter | solution.py:31
  14.0 31.9 %all_to_all.10 = bf16[4,2,128,512]{3,2,1,0:T(8,128)(2,1)S(1)} all-to-all(bf16[4,2,128,512]{3,2,1,0:T(8,128)(2,1)S(1)} %bitcast.34), channel_id=1, replica_groups=mesh['group'=2,'exp'=4,'tok'=4] {'exp'}, dimensions={0} | all-to-all | bytes 2097152 | tf_op jit(solution)/shard_map/all_to_all | solution.py:18
  45.8 0.0 copy-done
  45.8 0.0 copy-start.2
  45.8 1.7 %fusion.5 = bf16[4,2,128,512]{3,2,0,1:T(8,128)(2,1)} fusion(bf16[2,512,512]{2,1,0:T(8,128)(2,1)S(1)} %copy-done, bf16[4,2,128,512]{3,2,1,0:T(8,128)(2,1)S(1)} %all_to_all.10), kind=kOutput, calls=%fused_computation.12 | convolution fusion | flops 537395200 | bytes 3145728 | tf_op jit(solution)/shard_map/sxcf,xfh->sxch/dot_general | solution.py:34
  47.5 0.0 copy-done.2
  47.5 1.7 %fusion.6 = bf16[4,2,128,512]{3,2,0,1:T(8,128)(2,1)} fusion(bf16[2,512,512]{2,1,0:T(8,128)(2,1)S(1)} %copy-done.2, bf16[4,2,128,512]{3,2,1,0:T(8,128)(2,1)S(1)} %all_to_all.10), kind=kOutput, calls=%fused_computation.13 | convolution fusion | flops 537395200 | bytes 3145728 | tf_op jit(solution)/shard_map/sxcf,xfh->sxch/dot_general | solution.py:37
  49.2 0.0 all-reduce.3.cloned.1.call-update
  49.3 50.6 %all-reduce.3.cloned.1.call-done = (bf16[4,2,128,512]{3,2,0,1:T(8,128)(2,1)}, bf16[4,2,128,512]{3,2,0,1:T(8,128)(2,1)}) async-done(((bf16[4,2,128,512]{3,2,0,1:T(8,128)(2,1)}, bf16[4,2,128,512]{3,2,0,1:T(8,128)(2,1)}), (bf16[4,2,128,512]{3,2,0,1:T(8,128)(2,1)}, bf16[4,2,128,512]{3,2,0,1:T(8,128)(2,1)})) %all-reduce.3.cloned.1.call-update) | async-done | bytes 2097168 | tf_op jit(solution)/shard_map/psum | solution.py:40
  99.9 0.0 copy-done.3
  99.9 2.3 %fusion.7 = bf16[4,2,128,512]{3,2,0,1:T(8,128)(2,1)S(1)} fusion(bf16[2,512,512]{2,1,0:T(8,128)(2,1)S(1)} %copy-done.3, bf16[4,2,128,512]{3,2,0,1:T(8,128)(2,1)} %get-tuple-element.5, bf16[4,2,128,512]{3,2,0,1:T(8,128)(2,1)} %get-tuple-element.6), kind=kOutput, calls=%fused_computation.14 | convolution fusion | flops 541589504 | bytes 4194304 | tf_op jit(solution)/shard_map/sxch,xhf->sxcf/dot_general | solution.py:43
  102.3 1.1 copy.19
  103.4 4.7 %all-to-all-start.1 = ((bf16[4,2,128,512]{3,2,1,0:T(8,128)(2,1)}), bf16[4,2,128,512]{3,2,1,0:T(8,128)(2,1)S(1)}, u32[]{:S(2)}, u32[]{:S(2)}) async-start(bf16[4,2,128,512]{3,2,1,0:T(8,128)(2,1)} %copy.19), calls=%async_computation.1 | async-start | bytes 2097152 | tf_op jit(solution)/shard_map/all_to_all | solution.py:18
  108.1 0.0 copy-done.1
  108.1 0.1 copy.20
  108.2 25.4 %all-to-all-done.1 = bf16[4,2,128,512]{3,2,1,0:T(8,128)(2,1)S(1)} async-done(((bf16[4,2,128,512]{3,2,1,0:T(8,128)(2,1)}), bf16[4,2,128,512]{3,2,1,0:T(8,128)(2,1)S(1)}, u32[]{:S(2)}, u32[]{:S(2)}) %all-to-all-start.1) | async-done | bytes 1048608 | tf_op jit(solution)/shard_map/all_to_all | solution.py:18
  133.6 2.0 %gather_fusion = bf16[512,512]{1,0:T(8,128)(2,1)S(1)} fusion(bf16[1024,512]{1,0:T(8,128)(2,1)S(1)} %bitcast.33, s32[1024]{0:T(1024)S(1)} %pad_clamp_fusion), kind=kCustom, calls=%fused_computation | custom fusion | bytes 1050624 | tf_op jit(solution)/shard_map/gather | solution.py:47
  135.6 0.3 reshape.64
  135.9 1.4 multiply_reduce_fusion
  (7 shorter events, 0.1 us)
Async XLA Ops:
  6.5 39.3 %copy-start = (bf16[2,512,512]{2,1,0:T(8,128)(2,1)S(1)}, bf16[2,512,512]{2,1,0:T(8,128)(2,1)}, u32[]{:S(2)}) copy-start(bf16[2,512,512]{2,1,0:T(8,128)(2,1)} %param.9) | copy-start | bytes 3145732
  6.5 93.4 %all-reduce.3.cloned.1.call-start = ((), (), s32[]{:S(2)}) async-start(), calls=%async_computation.2 | async-start | bytes 4194304 | tf_op jit(solution)/shard_map/psum | solution.py:40
  45.8 1.7 %copy-start.2 = (bf16[2,512,512]{2,1,0:T(8,128)(2,1)S(1)}, bf16[2,512,512]{2,1,0:T(8,128)(2,1)}, u32[]{:S(2)}) copy-start(bf16[2,512,512]{2,1,0:T(8,128)(2,1)} %param.10) | copy-start | bytes 3145732
  49.2 50.7 %copy-start.3 = (bf16[2,512,512]{2,1,0:T(8,128)(2,1)S(1)}, bf16[2,512,512]{2,1,0:T(8,128)(2,1)}, u32[]{:S(2)}) copy-start(bf16[2,512,512]{2,1,0:T(8,128)(2,1)} %param.11) | copy-start | bytes 3145732
  103.4 4.7 %copy-start.1 = (f32[128,4]{0,1:T(4,128)S(1)}, f32[128,4]{0,1:T(4,128)}, u32[]{:S(2)}) copy-start(f32[128,4]{0,1:T(4,128)} %param.8) | copy-start | bytes 6148
  103.4 30.2 %all-to-all-start.1 = ((bf16[4,2,128,512]{3,2,1,0:T(8,128)(2,1)}), bf16[4,2,128,512]{3,2,1,0:T(8,128)(2,1)S(1)}, u32[]{:S(2)}, u32[]{:S(2)}) async-start(bf16[4,2,128,512]{3,2,1,0:T(8,128)(2,1)} %copy.19), calls=%async_computation.1 | async-start | bytes 2097152 | tf_op jit(solution)/shard_map/all_to_all | solution.py:18
Sparse Core Ops, SparseCore 0:
  49.4 50.4 all-reduce.2
where the time goes:
time: 144 us
  waiting for transfers between devices  76 us (53%)
  blocking collectives  31.9 us (22%)
  between operations  13.4 us (9%)
  local copies, waits for them, and re-layouts  8.96 us (6%)
  matrix products  5.73 us (4%)
  starting transfers between devices  4.73 us (3%)
  other arithmetic  3.33 us (2%)
    psum x1, waiting for transfers between devices, shards(): lax.psum(up_part.astype(jnp.bfloat16), 'tok').astype(jnp.float32)  50.6 us
    all_to_all x1, blocking collectives, move_rows(): lax.all_to_all(buffer, 'exp', split_axis=0, concat_axis=0, tiled=True)  31.9 us
    all_to_all x1, waiting for transfers between devices, move_rows(): lax.all_to_all(buffer, 'exp', split_axis=0, concat_axis=0, tiled=True)  25.4 us
    all_to_all x1, starting transfers between devices, move_rows(): lax.all_to_all(buffer, 'exp', split_axis=0, concat_axis=0, tiled=True)  4.73 us
  transfers between devices with their start and end apart: 2, of which 2 were waited for; matrix products, arithmetic and copies ran while one was open for 0% of the time, Pallas kernels for 0%

commit v1 on v0

--- a/solution.py
+++ b/solution.py
@@ -1,7 +1,16 @@
+import functools
 import jax
 import jax.numpy as jnp
 from jax import lax
 from jax.sharding import PartitionSpec as P
+
+
+def _define_map(field, row_axis):
+    r1 = lax.all_gather(field, axis_name=row_axis).sum(axis=0)
+    return r1
+
+
+draw_files = functools.partial(_define_map, row_axis="tok")
 
 
 def slot_positions(expert_ids, experts_all, capacity):
@@ -37,7 +46,7 @@
     up_part = jnp.einsum("sxcf,xfh->sxch", arrived, expert_up, preferred_element_type=jnp.float32)
     gate_pre, up_pre = (
         lax.psum(gate_part.astype(jnp.bfloat16), "tok").astype(jnp.float32),
-        lax.psum(up_part.astype(jnp.bfloat16), "tok").astype(jnp.float32),
+        draw_files(up_part.astype(jnp.bfloat16)).astype(jnp.float32),
     )
     hidden = (jax.nn.silu(gate_pre) * up_pre).astype(jnp.bfloat16)
     results = jnp.einsum(

time: 144 us -> 164 us (1.14)
  waiting for transfers between devices: 76 us -> 92.5 us
  other arithmetic: 3.33 us -> 6.43 us
    all_gather x0 -> x1, waiting for transfers between devices: none -> 31.9 us  [_define_map(): r1 = lax.all_gather(field, axis_name=row_axis).sum(axis=0)]
    psum x1, waiting for transfers between devices: 50.6 us -> 35.5 us  [shards(): lax.psum(gate_part.astype(jnp.bfloat16), 'tok').astype(jnp.float32)]
    reduce_sum x0 -> x1, other arithmetic: none -> 3.1 us  [_define_map(): r1 = lax.all_gather(field, axis_name=row_axis).sum(axis=0)]
  transfers between devices with their start and end apart: 2 -> 3, of which waited for: 2 -> 3; matrix products, arithmetic and copies ran while one was open for 0% -> 3% of each run, Pallas kernels for 0% -> 0%
where the time goes in v1:
time: 164 us; the launch traced here: 163 us
  waiting for transfers between devices  92.5 us (56%)
  blocking collectives  31.9 us (19%)
  between operations  13.5 us (8%)
  local copies, waits for them, and re-layouts  8.96 us (5%)
  other arithmetic  6.43 us (4%)
  matrix products  5.49 us (3%)
  starting transfers between devices  4.63 us (3%)
    psum x1, waiting for transfers between devices, shards(): lax.psum(gate_part.astype(jnp.bfloat16), 'tok').astype(jnp.float32)  35.5 us
    all_gather x1, waiting for transfers between devices, _define_map(): r1 = lax.all_gather(field, axis_name=row_axis).sum(axis=0)  31.9 us
    all_to_all x1, blocking collectives, move_rows(): lax.all_to_all(buffer, 'exp', split_axis=0, concat_axis=0, tiled=True)  31.9 us
    all_to_all x1, waiting for transfers between devices, move_rows(): lax.all_to_all(buffer, 'exp', split_axis=0, concat_axis=0, tiled=True)  25 us
    all_to_all x1, starting transfers between devices, move_rows(): lax.all_to_all(buffer, 'exp', split_axis=0, concat_axis=0, tiled=True)  4.59 us
  transfers between devices with their start and end apart: 3, of which 3 were waited for; matrix products, arithmetic and copies ran while one was open for 3% of the time, Pallas kernels for 0%

profile of v1, /device:TPU:0, one launch (start us, length us, event | category | flops | bytes accessed | tf_op | source)
XLA Modules:
  0.0 163.4 jit_solution(4618171611394560199)
XLA Ops:
  6.5 0.0 copy-start
  6.5 0.0 all-gather.3.cloned.1.call-start
  6.5 0.9 copy.15
  7.4 0.1 eq.29
  7.5 0.1 eq.25
  7.6 0.7 broadcast_multiply_fusion
  8.3 1.1 reduce-window.6
  9.5 0.2 slice_reduce_fusion
  9.7 0.1 copy.14
  9.8 0.1 mul.36
  9.9 1.0 broadcast_in_dim.5
  11.0 0.1 reshape.77
  11.1 0.1 fusion.17
  11.2 2.7 %scatter_custom_fusion = bf16[1024,512]{1,0:T(8,128)(2,1)S(1)} fusion(s32[512]{0:T(512)S(1)} %bitcast.37, bf16[512,512]{1,0:T(8,128)(2,1)S(1)} %reshape.77, bf16[]{:T(256)} %constant.6.clone.1), kind=kCustom, calls=%fused_computation.21 | custom fusion | bytes 1048578 | tf_op jit(solution)/shard_map/scatter | solution.py:40
  14.0 31.9 %all_to_all.10 = bf16[4,2,128,512]{3,2,1,0:T(8,128)(2,1)S(1)} all-to-all(bf16[4,2,128,512]{3,2,1,0:T(8,128)(2,1)S(1)} %bitcast.36), channel_id=1, replica_groups=mesh['group'=2,'exp'=4,'tok'=4] {'exp'}, dimensions={0} | all-to-all | bytes 2097152 | tf_op jit(solution)/shard_map/all_to_all | solution.py:27
  45.8 1.7 %fusion.6 = bf16[4,2,128,512]{3,2,0,1:T(8,128)(2,1)} fusion(bf16[2,512,512]{2,1,0:T(8,128)(2,1)S(1)} %copy-done, bf16[4,2,128,512]{3,2,1,0:T(8,128)(2,1)S(1)} %all_to_all.10), kind=kOutput, calls=%fused_computation.13 | convolution fusion | flops 537395200 | bytes 3145728 | tf_op jit(solution)/shard_map/sxcf,xfh->sxch/dot_general | solution.py:46
  47.6 0.0 all-gather.3.cloned.1.call-update
  47.6 0.0 all-reduce.2.cloned.1.call-start
  47.7 1.7 %fusion.5 = bf16[4,2,128,512]{3,2,0,1:T(8,128)(2,1)} fusion(bf16[2,512,512]{2,1,0:T(8,128)(2,1)S(1)} %copy-done.2, bf16[4,2,128,512]{3,2,1,0:T(8,128)(2,1)S(1)} %all_to_all.10), kind=kOutput, calls=%fused_computation.12 | convolution fusion | flops 537395200 | bytes 3145728 | tf_op jit(solution)/shard_map/sxcf,xfh->sxch/dot_general | solution.py:43
  49.4 0.0 all-reduce.2.cloned.1.call-update
  49.4 31.9 %all-gather.3.cloned.1.call-done = bf16[16,2,128,512]{3,2,0,1:T(8,128)(2,1)} async-done(((bf16[4,2,128,512]{3,2,0,1:T(8,128)(2,1)}), bf16[16,2,128,512]{3,2,0,1:T(8,128)(2,1)}) %all-gather.3.cloned.1.call-update) | async-done | bytes 4194320 | tf_op jit(solution)/shard_map/all_gather | solution.py:9
  81.3 3.1 %reduce_sum.34 = bf16[4,2,128,512]{3,2,0,1:T(8,128)(2,1)S(1)} reduce(bf16[4,4,2,128,512]{4,3,1,0,2:T(8,128)(2,1)} %bitcast.35, bf16[]{:T(256)} %constant.6.clone.1), dimensions={0}, to_apply=%region_5.6 | reduce | flops 1572864 | bytes 5242882 | tf_op jit(solution)/shard_map/reduce_sum | solution.py:9
  84.4 35.5 %all-reduce.2.cloned.1.call-done = bf16[4,2,128,512]{3,2,0,1:T(8,128)(2,1)} async-done(((bf16[4,2,128,512]{3,2,0,1:T(8,128)(2,1)}), bf16[4,2,128,512]{3,2,0,1:T(8,128)(2,1)}) %all-reduce.2.cloned.1.call-update) | async-done | bytes 1048592 | tf_op jit(solution)/shard_map/psum | solution.py:48
  120.0 2.0 %fusion.7 = bf16[4,2,128,512]{3,2,0,1:T(8,128)(2,1)S(1)} fusion(bf16[2,512,512]{2,1,0:T(8,128)(2,1)S(1)} %copy-done.3, bf16[4,2,128,512]{3,2,0,1:T(8,128)(2,1)S(1)} %reduce_sum.34, bf16[4,2,128,512]{3,2,0,1:T(8,128)(2,1)} %all-reduce.2.cloned.1.call-done), kind=kOutput, calls=%fused_computation.14 | convolution fusion | flops 541589504 | bytes 4194304 | tf_op jit(solution)/shard_map/sxch,xhf->sxcf/dot_general | solution.py:52
  122.0 0.0 copy-start.1
  122.0 1.1 copy.19
  123.1 4.6 %all-to-all-start.1 = ((bf16[4,2,128,512]{3,2,1,0:T(8,128)(2,1)}), bf16[4,2,128,512]{3,2,1,0:T(8,128)(2,1)S(1)}, u32[]{:S(2)}, u32[]{:S(2)}) async-start(bf16[4,2,128,512]{3,2,1,0:T(8,128)(2,1)} %copy.19), calls=%async_computation.1 | async-start | bytes 2097152 | tf_op jit(solution)/shard_map/all_to_all | solution.py:27
  127.7 0.1 copy.20
  127.9 25.0 %all-to-all-done.1 = bf16[4,2,128,512]{3,2,1,0:T(8,128)(2,1)S(1)} async-done(((bf16[4,2,128,512]{3,2,1,0:T(8,128)(2,1)}), bf16[4,2,128,512]{3,2,1,0:T(8,128)(2,1)S(1)}, u32[]{:S(2)}, u32[]{:S(2)}) %all-to-all-start.1) | async-done | bytes 1048608 | tf_op jit(solution)/shard_map/all_to_all | solution.py:27
  152.9 2.0 %gather_fusion = bf16[512,512]{1,0:T(8,128)(2,1)S(1)} fusion(bf16[1024,512]{1,0:T(8,128)(2,1)S(1)} %bitcast.34, s32[1024]{0:T(1024)S(1)} %pad_clamp_fusion), kind=kCustom, calls=%fused_computation | custom fusion | bytes 1050624 | tf_op jit(solution)/shard_map/gather | solution.py:56
  154.9 0.3 reshape.64
  155.2 1.4 multiply_reduce_fusion
  (11 shorter events, 0.1 us)
Async XLA Ops:
  6.5 39.3 %copy-start = (bf16[2,512,512]{2,1,0:T(8,128)(2,1)S(1)}, bf16[2,512,512]{2,1,0:T(8,128)(2,1)}, u32[]{:S(2)}) copy-start(bf16[2,512,512]{2,1,0:T(8,128)(2,1)} %param.10) | copy-start | bytes 3145732
  6.5 74.8 %all-gather.3.cloned.1.call-start = ((), (), s32[]{:S(2)}) async-start(), calls=%async_computation.3 | async-start | bytes 5242880 | tf_op jit(solution)/shard_map/all_gather | solution.py:9
  45.8 1.8 %copy-start.2 = (bf16[2,512,512]{2,1,0:T(8,128)(2,1)S(1)}, bf16[2,512,512]{2,1,0:T(8,128)(2,1)}, u32[]{:S(2)}) copy-start(bf16[2,512,512]{2,1,0:T(8,128)(2,1)} %param.9) | copy-start | bytes 3145732
  47.6 72.4 %all-reduce.2.cloned.1.call-start = ((), (), s32[]{:S(2)}) async-start(), calls=%async_computation.2 | async-start | bytes 2097152 | tf_op jit(solution)/shard_map/psum | solution.py:48
  81.3 38.7 %copy-start.3 = (bf16[2,512,512]{2,1,0:T(8,128)(2,1)S(1)}, bf16[2,512,512]{2,1,0:T(8,128)(2,1)}, u32[]{:S(2)}) copy-start(bf16[2,512,512]{2,1,0:T(8,128)(2,1)} %param.11) | copy-start | bytes 3145732
  122.0 5.7 %copy-start.1 = (f32[128,4]{0,1:T(4,128)S(1)}, f32[128,4]{0,1:T(4,128)}, u32[]{:S(2)}) copy-start(f32[128,4]{0,1:T(4,128)} %param.8) | copy-start | bytes 6148
  123.1 29.7 %all-to-all-start.1 = ((bf16[4,2,128,512]{3,2,1,0:T(8,128)(2,1)}), bf16[4,2,128,512]{3,2,1,0:T(8,128)(2,1)S(1)}, u32[]{:S(2)}, u32[]{:S(2)}) async-start(bf16[4,2,128,512]{3,2,1,0:T(8,128)(2,1)} %copy.19), calls=%async_computation.1 | async-start | bytes 2097152 | tf_op jit(solution)/shard_map/all_to_all | solution.py:27
Sparse Core Ops, SparseCore 0:
  47.7 33.5 all-gather.2
  83.7 36.2 all-reduce.1
